TPU v7x, 512 devices: a whole 4x4x16 slice. The times are simulated.
512 devices in a mesh: row: 32 (over x, z_lo, core), col: 16 (over y, z_hi).
Axes of the slice: x: 4, y: 4, z: 16 (z_hi: 4, z_lo: 4; z = z_hi * 4 + z_lo), core: 2. Of those that a mesh axis runs over, the one named last changes fastest.
Arguments:
- amplitudes: bfloat16 [2, 2048, 2048], P(None, 'row', 'col'), may hold values from -6 to 6
- factor: bfloat16 [2048, 4096], P('row', 'col'), may hold values from -0.125 to 0.125
- kernel: float32 [4096, 4096], P('row', 'col'), may hold values from -6 to 6
Outputs:
- ladder: bfloat16 [2, 2048, 2048], P(None, 'row', 'col')
All inputs are finite; a program needn't handle non-finite values.
Results may differ from a plain program's by a relative error of at most 0.015.
Values may be sent and summed in bfloat16 or wider, within the bound.
A program may use at most 64 MiB of HBM per device.

v0:
```python
import jax
import jax.numpy as jnp
from jax import lax
from jax.sharding import PartitionSpec as P


def in_order(parts, dim):
    parts = jnp.moveaxis(parts, 0, dim)
    shape = parts.shape
    return parts.reshape(*shape[:dim], shape[dim] * shape[dim + 1], *shape[dim + 2 :])


def sent_to_all(value, axis):
    copies = jnp.broadcast_to(value, (lax.axis_size(axis), *value.shape))
    return lax.all_to_all(copies, axis, split_axis=0, concat_axis=0, tiled=True)


def gathered_copies(value, axis, dim):
    return in_order(sent_to_all(value, axis), dim)


def cut_along(value, dim, size):
    shape = value.shape
    parts = value.reshape(*shape[:dim], size, shape[dim] // size, *shape[dim + 1 :])
    return jnp.moveaxis(parts, dim, 0)


def sent_and_summed(value, axis, dim):
    size = lax.axis_size(axis)
    parts = lax.all_to_all(cut_along(value, dim, size), axis, 0, 0, tiled=True)
    return jnp.sum(parts.astype(jnp.float32), axis=0)


def per_device(amplitudes, factor, kernel):
    factor_cols = gathered_copies(factor, "row", 0)
    factor_rows = gathered_copies(factor, "col", 1)
    factor_first = lax.all_to_all(factor_rows, "row", split_axis=1, concat_axis=0, tiled=True)
    factor_part = factor_cols
    projected = jnp.einsum(
        "pak,kq->paq",
        gathered_copies(amplitudes, "col", 2),
        factor_part,
        preferred_element_type=jnp.float32,
    ).astype(jnp.bfloat16)
    factor_part = factor_first
    grid_pairs = jnp.einsum(
        "kp,nkq->npq",
        factor_part,
        gathered_copies(projected, "row", 1),
        preferred_element_type=jnp.float32,
    )
    scaled = (kernel[None] * grid_pairs).astype(jnp.bfloat16)
    factor_part = factor_cols
    half_back = sent_and_summed(
        jnp.einsum("bq,npq->bnp", factor_part, scaled, preferred_element_type=jnp.float32).astype(
            jnp.bfloat16
        ),
        "col",
        0,
    )
    half_back = half_back.astype(jnp.bfloat16)
    factor_part = factor_rows
    result = jnp.einsum(
        "ak,bnk->nab",
        factor_part,
        gathered_copies(half_back, "row", 2),
        preferred_element_type=jnp.float32,
    )
    return result.astype(jnp.bfloat16)


def solution(mesh):
    placed = (P(None, "row", "col"), P("row", "col"), P("row", "col"))
    return jax.shard_map(
        per_device, mesh=mesh, in_specs=placed, out_specs=P(None, "row", "col"), check_vma=False
    )
```

profile of v0, /device:TPU:1, one launch (start us, length us, event | category | flops | bytes accessed | tf_op | source)
XLA Modules:
  0.0 323.4 jit_solution(5627007424775163365)
XLA Ops:
  0.0 0.9 broadcast_in_dim.16
  0.9 45.3 %all_to_all.46 = bf16[16,2,64,128]{3,2,1,0:T(8,128)(2,1)S(1)} all-to-all(bf16[16,2,64,128]{3,2,1,0:T(8,128)(2,1)S(1)} %broadcast_in_dim.16), channel_id=1, replica_groups=mesh['row'=32,'col'=16] {'col'}, dimensions={0} | all-to-all | bytes 1048576 | tf_op jit(solution)/shard_map/all_to_all | solution.py:15
  46.2 0.8 broadcast_in_dim.19
  47.0 29.1 %all_to_all.47 = bf16[16,64,256]{2,1,0:T(8,128)(2,1)S(1)} all-to-all(bf16[16,64,256]{2,1,0:T(8,128)(2,1)S(1)} %broadcast_in_dim.19), channel_id=1, replica_groups=mesh['row'=32,'col'=16] {'col'}, dimensions={0} | all-to-all | bytes 1048576 | tf_op jit(solution)/shard_map/all_to_all | solution.py:15
  76.1 0.0 copy-done.3
  76.1 1.1 broadcast_in_dim.17
  77.2 21.4 %all-to-all-start.1 = ((bf16[32,64,256]{2,1,0:T(8,128)(2,1)}), bf16[32,64,256]{2,1,0:T(8,128)(2,1)S(1)}, u32[]{:S(2)}, u32[]{:S(2)}) async-start(bf16[32,64,256]{2,1,0:T(8,128)(2,1)} %broadcast_in_dim.17), calls=%async_computation.1 | async-start | bytes 2097152 | tf_op jit(solution)/shard_map/all_to_all | solution.py:15
  98.6 0.3 copy.14
  98.9 0.0 copy-start
  98.9 0.2 all_to_all.34
  99.1 1.0 copy.15
  100.1 26.3 %all-to-all-done.1 = bf16[32,64,256]{2,1,0:T(8,128)(2,1)S(1)} async-done(((bf16[32,64,256]{2,1,0:T(8,128)(2,1)}), bf16[32,64,256]{2,1,0:T(8,128)(2,1)S(1)}, u32[]{:S(2)}, u32[]{:S(2)}) %all-to-all-start.1) | async-done | bytes 1048608 | tf_op jit(solution)/shard_map/all_to_all | solution.py:15
  126.4 3.9 %all-to-all-start.4 = ((bf16[64,32,128]{2,0,1:T(8,128)(2,1)}), bf16[64,32,128]{2,0,1:T(8,128)(2,1)S(1)}, u32[]{:S(2)}, u32[]{:S(2)}) async-start(bf16[64,32,128]{2,0,1:T(8,128)(2,1)} %copy.15), calls=%async_computation.4 | async-start | bytes 1048576 | tf_op jit(solution)/shard_map/all_to_all | solution.py:37
  130.3 0.3 convolution_convert_fusion.1
  130.6 0.0 copy-done
  130.6 16.5 %all-to-all-done.4 = bf16[64,32,128]{2,0,1:T(8,128)(2,1)S(1)} async-done(((bf16[64,32,128]{2,0,1:T(8,128)(2,1)}), bf16[64,32,128]{2,0,1:T(8,128)(2,1)S(1)}, u32[]{:S(2)}, u32[]{:S(2)}) %all-to-all-start.4) | async-done | bytes 524320 | tf_op jit(solution)/shard_map/all_to_all | solution.py:37
  147.1 1.6 broadcast_in_dim.18
  148.7 0.0 copy-done.2
  148.7 3.9 %all-to-all-start.2 = ((bf16[32,2,64,256]{3,2,1,0:T(8,128)(2,1)}), bf16[32,2,64,256]{3,2,1,0:T(8,128)(2,1)S(1)}, u32[]{:S(2)}, u32[]{:S(2)}) async-start(bf16[32,2,64,256]{3,2,1,0:T(8,128)(2,1)} %broadcast_in_dim.18), calls=%async_computation.2 | async-start | bytes 4194304 | tf_op jit(solution)/shard_map/all_to_all | solution.py:15
  152.6 0.0 copy-done.4
  152.6 0.1 copy.12
  152.7 49.8 %all-to-all-done.2 = bf16[32,2,64,256]{3,2,1,0:T(8,128)(2,1)S(1)} async-done(((bf16[32,2,64,256]{3,2,1,0:T(8,128)(2,1)}), bf16[32,2,64,256]{3,2,1,0:T(8,128)(2,1)S(1)}, u32[]{:S(2)}, u32[]{:S(2)}) %all-to-all-start.2) | async-done | bytes 2097184 | tf_op jit(solution)/shard_map/all_to_all | solution.py:15
  202.5 3.7 %fusion.5 = bf16[2,16,16,8,128]{4,3,2,1,0:T(8,128)(2,1)} fusion(bf16[2048,256,1]{1,0,2:T(8,128)(2,1)S(1)} %bitcast.65, bf16[32,2,64,256]{3,2,1,0:T(8,128)(2,1)S(1)} %all-to-all-done.2, bf16[64,32,128]{2,0,1:T(8,128)(2,1)} %copy-done.2, f32[128,256]{0,1:T(8,128)S(1)} %copy.12), kind=kOutput, calls=%fused_computation.6 | convolution fusion | flops 537526272 | bytes 4849664 | tf_op jit(solution)/shard_map/bq,npq->bnp/dot_general | solution.py:55
  206.2 1.5 copy.41
  207.7 56.5 %all_to_all.48 = bf16[16,128,2,128]{1,3,2,0:T(8,128)(2,1)S(1)} all-to-all(bf16[16,128,2,128]{1,3,2,0:T(8,128)(2,1)S(1)} %bitcast.66), channel_id=1, replica_groups=mesh['row'=32,'col'=16] {'col'}, dimensions={0} | all-to-all | bytes 2097152 | tf_op jit(solution)/shard_map/all_to_all | solution.py:30
  264.2 0.1 reduce_sum.12
  264.3 0.1 copy.19
  264.4 1.8 broadcast_in_dim.20
  266.3 5.8 %all-to-all-start.6 = ((bf16[32,128,2,128]{3,1,2,0:T(8,128)(2,1)}), bf16[32,128,2,128]{3,1,2,0:T(8,128)(2,1)S(1)}, u32[]{:S(2)}, u32[]{:S(2)}) async-start(bf16[32,128,2,128]{3,1,2,0:T(8,128)(2,1)} %broadcast_in_dim.20), calls=%async_computation.6 | async-start | bytes 4194304 | tf_op jit(solution)/shard_map/all_to_all | solution.py:15
  272.1 0.2 reshape.29
  272.4 49.6 %all-to-all-done.6 = bf16[32,128,2,128]{3,1,2,0:T(8,128)(2,1)S(1)} async-done(((bf16[32,128,2,128]{3,1,2,0:T(8,128)(2,1)}), bf16[32,128,2,128]{3,1,2,0:T(8,128)(2,1)S(1)}, u32[]{:S(2)}, u32[]{:S(2)}) %all-to-all-start.6) | async-done | bytes 2097184 | tf_op jit(solution)/shard_map/all_to_all | solution.py:15
  322.0 1.4 fusion.18
  (5 shorter events, 0.0 us)
Async XLA Ops:
  0.0 76.1 %copy-start.3 = (bf16[64,256]{1,0:T(8,128)(2,1)S(1)}, bf16[64,256]{1,0:T(8,128)(2,1)}, u32[]{:S(2)}) copy-start(bf16[64,256]{1,0:T(8,128)(2,1)} %param.4) | copy-start | bytes 98308
  77.2 49.2 %all-to-all-start.1 = ((bf16[32,64,256]{2,1,0:T(8,128)(2,1)}), bf16[32,64,256]{2,1,0:T(8,128)(2,1)S(1)}, u32[]{:S(2)}, u32[]{:S(2)}) async-start(bf16[32,64,256]{2,1,0:T(8,128)(2,1)} %broadcast_in_dim.17), calls=%async_computation.1 | async-start | bytes 2097152 | tf_op jit(solution)/shard_map/all_to_all | solution.py:15
  98.9 31.7 %copy-start = (bf16[64,16,256]{2,1,0:T(8,128)(2,1)}, bf16[64,16,256]{2,1,0:T(8,128)(2,1)S(1)}, u32[]{:S(2)}) copy-start(bf16[64,16,256]{2,1,0:T(8,128)(2,1)S(1)} %copy.14) | copy-start | bytes 1572868
  126.4 20.7 %all-to-all-start.4 = ((bf16[64,32,128]{2,0,1:T(8,128)(2,1)}), bf16[64,32,128]{2,0,1:T(8,128)(2,1)S(1)}, u32[]{:S(2)}, u32[]{:S(2)}) async-start(bf16[64,32,128]{2,0,1:T(8,128)(2,1)} %copy.15), calls=%async_computation.4 | async-start | bytes 1048576 | tf_op jit(solution)/shard_map/all_to_all | solution.py:37
  147.1 1.6 copy-start.2
  148.7 3.9 %copy-start.4 = (f32[128,256]{1,0:T(8,128)S(1)}, f32[128,256]{1,0:T(8,128)}, u32[]{:S(2)}) copy-start(f32[128,256]{1,0:T(8,128)} %param.5) | copy-start | bytes 393220
  148.7 53.8 %all-to-all-start.2 = ((bf16[32,2,64,256]{3,2,1,0:T(8,128)(2,1)}), bf16[32,2,64,256]{3,2,1,0:T(8,128)(2,1)S(1)}, u32[]{:S(2)}, u32[]{:S(2)}) async-start(bf16[32,2,64,256]{3,2,1,0:T(8,128)(2,1)} %broadcast_in_dim.18), calls=%async_computation.2 | async-start | bytes 4194304 | tf_op jit(solution)/shard_map/all_to_all | solution.py:15
  266.3 5.8 %copy-start.1 = (bf16[64,16,256]{2,1,0:T(8,128)(2,1)S(1)}, bf16[64,16,256]{2,1,0:T(8,128)(2,1)}, u32[]{:S(2)}) copy-start(bf16[64,16,256]{2,1,0:T(8,128)(2,1)} %copy-done) | copy-start | bytes 1572868
  266.3 55.7 %all-to-all-start.6 = ((bf16[32,128,2,128]{3,1,2,0:T(8,128)(2,1)}), bf16[32,128,2,128]{3,1,2,0:T(8,128)(2,1)S(1)}, u32[]{:S(2)}, u32[]{:S(2)}) async-start(bf16[32,128,2,128]{3,1,2,0:T(8,128)(2,1)} %broadcast_in_dim.20), calls=%async_computation.6 | async-start | bytes 4194304 | tf_op jit(solution)/shard_map/all_to_all | solution.py:15
where the time goes:
time: 324 us; the launch traced here: 323 us
  waiting for transfers between devices  142 us (44%)
  blocking collectives  131 us (40%)
  starting transfers between devices  35 us (11%)
  local copies, waits for them, and re-layouts  9.69 us (3%)
  matrix products  5.35 us (2%)
    all_to_all x3, waiting for transfers between devices, sent_to_all(): return lax.all_to_all(copies, axis, split_axis=0, concat_axis=0, tiled=True)  126 us
    all_to_all x2, blocking collectives, sent_to_all(): return lax.all_to_all(copies, axis, split_axis=0, concat_axis=0, tiled=True)  74.4 us
    all_to_all x1, blocking collectives, sent_and_summed(): parts = lax.all_to_all(cut_along(value, dim, size), axis, 0, 0, tiled=True)  56.5 us
    all_to_all x3, starting transfers between devices, sent_to_all(): return lax.all_to_all(copies, axis, split_axis=0, concat_axis=0, tiled=True)  31.1 us
    all_to_all x1, waiting for transfers between devices, per_device(): lax.all_to_all(factor_rows, 'row', split_axis=1, concat_axis=0, tiled=True)  16.5 us
  transfers between devices with their start and end apart: 4, of which 4 were waited for; matrix products, arithmetic and copies ran while one was open for 1% of the time, Pallas kernels for 0%

commit v1 on v0

--- a/solution.py
+++ b/solution.py
@@ -34,7 +34,10 @@
 def per_device(amplitudes, factor, kernel):
     factor_cols = gathered_copies(factor, "row", 0)
     factor_rows = gathered_copies(factor, "col", 1)
-    factor_first = lax.all_to_all(factor_rows, "row", split_axis=1, concat_axis=0, tiled=True)
+    factor_first = jnp.concatenate(
+        lax.all_to_all(jnp.stack(jnp.split(factor_rows, lax.axis_size("row"), 1), 0), "row", 0, 0),
+        0,
+    )
     factor_part = factor_cols
     projected = jnp.einsum(
         "pak,kq->paq",

time: 324 us -> 325 us (level)
  blocking collectives: 131 us -> 102 us
  local copies, waits for them, and re-layouts: 9.69 us -> 28.6 us
  starting transfers between devices: 35 us -> 43.6 us
    all_to_all x2 -> x1, blocking collectives: 74.4 us -> 45.3 us  [sent_to_all(): return lax.all_to_all(copies, axis, split_axis=0, concat_axis=0, tiled=True)]
    unnamed x11 -> x42, local copies, waits for them, and re-layouts: 0.11 us -> 18.8 us
    all_to_all x3 -> x4, starting transfers between devices: 31.1 us -> 39.7 us  [sent_to_all(): return lax.all_to_all(copies, axis, split_axis=0, concat_axis=0, tiled=True)]
    all_to_all x3 -> x4, waiting for transfers between devices: 126 us -> 128 us  [sent_to_all(): return lax.all_to_all(copies, axis, split_axis=0, concat_axis=0, tiled=True)]
  transfers between devices with their start and end apart: 4 -> 5, of which waited for: 4 -> 5; matrix products, arithmetic and copies ran while one was open for 1% -> 6% of each run, Pallas kernels for 0% -> 0%
where the time goes in v1:
time: 325 us; the launch traced here: 324 us
  waiting for transfers between devices  145 us (45%)
  blocking collectives  102 us (31%)
  starting transfers between devices  43.6 us (13%)
  local copies, waits for them, and re-layouts  28.6 us (9%)
  matrix products  5.35 us (2%)
    all_to_all x4, waiting for transfers between devices, sent_to_all(): return lax.all_to_all(copies, axis, split_axis=0, concat_axis=0, tiled=True)  128 us
    all_to_all x1, blocking collectives, sent_and_summed(): parts = lax.all_to_all(cut_along(value, dim, size), axis, 0, 0, tiled=True)  56.5 us
    all_to_all x1, blocking collectives, sent_to_all(): return lax.all_to_all(copies, axis, split_axis=0, concat_axis=0, tiled=True)  45.3 us
    all_to_all x4, starting transfers between devices, sent_to_all(): return lax.all_to_all(copies, axis, split_axis=0, concat_axis=0, tiled=True)  39.7 us
    unnamed x42, local copies, waits for them, and re-layouts  18.8 us
    all_to_all x1, waiting for transfers between devices, per_device(): lax.all_to_all(jnp.stack(jnp.split(factor_rows, lax.axis_size('row'), 1),...  16.5 us
    broadcast_in_dim x5, local copies, waits for them, and re-layouts, sent_to_all(): copies = jnp.broadcast_to(value, (lax.axis_size(axis), *value.shape))  7 us
  transfers between devices with their start and end apart: 5, of which 5 were waited for; matrix products, arithmetic and copies ran while one was open for 6% of the time, Pallas kernels for 0%

profile of v1, /device:TPU:1, one launch (start us, length us, event | category | flops | bytes accessed | tf_op | source)
XLA Modules:
  0.0 324.4 jit_solution(2200252400978301048)
XLA Ops:
  0.0 0.8 broadcast_in_dim.19
  0.8 45.3 %all_to_all.35 = bf16[16,64,256]{2,1,0:T(8,128)(2,1)S(1)} all-to-all(bf16[16,64,256]{2,1,0:T(8,128)(2,1)S(1)} %broadcast_in_dim.19), channel_id=1, replica_groups=mesh['row'=32,'col'=16] {'col'}, dimensions={0} | all-to-all | bytes 1048576 | tf_op jit(solution)/shard_map/all_to_all | solution.py:15
  46.1 1.7 broadcast_in_dim.16
  47.8 8.6 %all-to-all-start = ((bf16[16,2,64,128]{3,2,1,0:T(8,128)(2,1)}), bf16[16,2,64,128]{3,2,1,0:T(8,128)(2,1)S(1)}, u32[]{:S(2)}, u32[]{:S(2)}) async-start(bf16[16,2,64,128]{3,2,1,0:T(8,128)(2,1)} %broadcast_in_dim.16), calls=%async_computation | async-start | bytes 1048576 | tf_op jit(solution)/shard_map/all_to_all | solution.py:15
  57.1 0.6 constant_dynamic-update-slice_fusion.30
  59.5 0.6 constant_dynamic-update-slice_fusion.26
  60.1 0.6 constant_dynamic-update-slice_fusion.25
  60.7 0.6 constant_dynamic-update-slice_fusion.24
  61.9 0.6 constant_dynamic-update-slice_fusion.22
  64.3 12.8 %all-to-all-done = bf16[16,2,64,128]{3,2,1,0:T(8,128)(2,1)S(1)} async-done(((bf16[16,2,64,128]{3,2,1,0:T(8,128)(2,1)}), bf16[16,2,64,128]{3,2,1,0:T(8,128)(2,1)S(1)}, u32[]{:S(2)}, u32[]{:S(2)}) %all-to-all-start) | async-done | bytes 524320 | tf_op jit(solution)/shard_map/all_to_all | solution.py:15
  77.1 1.1 broadcast_in_dim.17
  78.2 21.4 %all-to-all-start.1 = ((bf16[32,64,256]{2,1,0:T(8,128)(2,1)}), bf16[32,64,256]{2,1,0:T(8,128)(2,1)S(1)}, u32[]{:S(2)}, u32[]{:S(2)}) async-start(bf16[32,64,256]{2,1,0:T(8,128)(2,1)} %broadcast_in_dim.17), calls=%async_computation.1 | async-start | bytes 2097152 | tf_op jit(solution)/shard_map/all_to_all | solution.py:15
  100.2 0.6 constant_dynamic-update-slice_fusion.17
  102.0 0.6 constant_dynamic-update-slice_fusion.14
  102.6 0.6 constant_dynamic-update-slice_fusion.13
  105.7 0.6 constant_dynamic-update-slice_fusion.8
  106.9 0.6 constant_dynamic-update-slice_fusion.6
  107.5 0.6 constant_dynamic-update-slice_fusion.5
  108.7 0.6 constant_dynamic-update-slice_fusion.3
  111.1 16.4 %all-to-all-done.1 = bf16[32,64,256]{2,1,0:T(8,128)(2,1)S(1)} async-done(((bf16[32,64,256]{2,1,0:T(8,128)(2,1)}), bf16[32,64,256]{2,1,0:T(8,128)(2,1)S(1)}, u32[]{:S(2)}, u32[]{:S(2)}) %all-to-all-start.1) | async-done | bytes 1048608 | tf_op jit(solution)/shard_map/all_to_all | solution.py:15
  127.5 3.9 %all-to-all-start.4 = ((bf16[32,64,128]{2,1,0:T(8,128)(2,1)}), bf16[32,64,128]{2,1,0:T(8,128)(2,1)S(1)}, u32[]{:S(2)}, u32[]{:S(2)}) async-start(bf16[32,64,128]{2,1,0:T(8,128)(2,1)} %constant_dynamic-update-slice_fusion), calls=%async_computation.4 | async-start | bytes 1048576 | tf_op jit(solution)/shard_map/all_to_all | solution.py:38
  131.6 16.5 %all-to-all-done.4 = bf16[32,64,128]{2,1,0:T(8,128)(2,1)S(1)} async-done(((bf16[32,64,128]{2,1,0:T(8,128)(2,1)}), bf16[32,64,128]{2,1,0:T(8,128)(2,1)S(1)}, u32[]{:S(2)}, u32[]{:S(2)}) %all-to-all-start.4) | async-done | bytes 524320 | tf_op jit(solution)/shard_map/all_to_all | solution.py:38
  148.1 1.6 broadcast_in_dim.18
  149.7 3.9 %all-to-all-start.2 = ((bf16[32,2,64,256]{3,2,1,0:T(8,128)(2,1)}), bf16[32,2,64,256]{3,2,1,0:T(8,128)(2,1)S(1)}, u32[]{:S(2)}, u32[]{:S(2)}) async-start(bf16[32,2,64,256]{3,2,1,0:T(8,128)(2,1)} %broadcast_in_dim.18), calls=%async_computation.2 | async-start | bytes 4194304 | tf_op jit(solution)/shard_map/all_to_all | solution.py:15
  153.8 49.8 %all-to-all-done.2 = bf16[32,2,64,256]{3,2,1,0:T(8,128)(2,1)S(1)} async-done(((bf16[32,2,64,256]{3,2,1,0:T(8,128)(2,1)}), bf16[32,2,64,256]{3,2,1,0:T(8,128)(2,1)S(1)}, u32[]{:S(2)}, u32[]{:S(2)}) %all-to-all-start.2) | async-done | bytes 2097184 | tf_op jit(solution)/shard_map/all_to_all | solution.py:15
  203.5 3.7 %fusion.5 = bf16[2,16,16,8,128]{4,3,2,1,0:T(8,128)(2,1)} fusion(bf16[2048,256,1]{1,0,2:T(8,128)(2,1)S(1)} %bitcast.193, bf16[32,2,64,256]{3,2,1,0:T(8,128)(2,1)S(1)} %all-to-all-done.2, bf16[32,64,128]{2,1,0:T(8,128)(2,1)} %copy-done.2, f32[128,256]{0,1:T(8,128)S(1)} %copy.4), kind=kOutput, calls=%fused_computation.6 | convolution fusion | flops 537526272 | bytes 4849664 | tf_op jit(solution)/shard_map/bq,npq->bnp/dot_general | solution.py:58
  207.2 1.5 copy.32
  208.7 56.5 %all_to_all.36 = bf16[16,128,2,128]{1,3,2,0:T(8,128)(2,1)S(1)} all-to-all(bf16[16,128,2,128]{1,3,2,0:T(8,128)(2,1)S(1)} %bitcast.196), channel_id=1, replica_groups=mesh['row'=32,'col'=16] {'col'}, dimensions={0} | all-to-all | bytes 2097152 | tf_op jit(solution)/shard_map/all_to_all | solution.py:30
  265.5 1.8 broadcast_in_dim.20
  267.3 5.8 %all-to-all-start.6 = ((bf16[32,128,2,128]{3,1,2,0:T(8,128)(2,1)}), bf16[32,128,2,128]{3,1,2,0:T(8,128)(2,1)S(1)}, u32[]{:S(2)}, u32[]{:S(2)}) async-start(bf16[32,128,2,128]{3,1,2,0:T(8,128)(2,1)} %broadcast_in_dim.20), calls=%async_computation.6 | async-start | bytes 4194304 | tf_op jit(solution)/shard_map/all_to_all | solution.py:15
  273.7 49.3 %all-to-all-done.6 = bf16[32,128,2,128]{3,1,2,0:T(8,128)(2,1)S(1)} async-done(((bf16[32,128,2,128]{3,1,2,0:T(8,128)(2,1)}), bf16[32,128,2,128]{3,1,2,0:T(8,128)(2,1)S(1)}, u32[]{:S(2)}, u32[]{:S(2)}) %all-to-all-start.6) | async-done | bytes 2097184 | tf_op jit(solution)/shard_map/all_to_all | solution.py:15
  323.0 1.4 fusion.18
  (37 shorter events, 13.3 us)
Async XLA Ops:
  0.8 76.3 %copy-start.3 = (bf16[64,256]{1,0:T(8,128)(2,1)S(1)}, bf16[64,256]{1,0:T(8,128)(2,1)}, u32[]{:S(2)}) copy-start(bf16[64,256]{1,0:T(8,128)(2,1)} %param.4) | copy-start | bytes 98308
  46.1 32.1 %copy-start = (bf16[16,64,256]{2,1,0:T(8,128)(2,1)}, bf16[16,64,256]{2,1,0:T(8,128)(2,1)S(1)}, u32[]{:S(2)}) copy-start(bf16[16,64,256]{2,1,0:T(8,128)(2,1)S(1)} %all_to_all.35) | copy-start | bytes 1572868
  47.8 29.3 %all-to-all-start = ((bf16[16,2,64,128]{3,2,1,0:T(8,128)(2,1)}), bf16[16,2,64,128]{3,2,1,0:T(8,128)(2,1)S(1)}, u32[]{:S(2)}, u32[]{:S(2)}) async-start(bf16[16,2,64,128]{3,2,1,0:T(8,128)(2,1)} %broadcast_in_dim.16), calls=%async_computation | async-start | bytes 1048576 | tf_op jit(solution)/shard_map/all_to_all | solution.py:15
  78.2 49.2 %all-to-all-start.1 = ((bf16[32,64,256]{2,1,0:T(8,128)(2,1)}), bf16[32,64,256]{2,1,0:T(8,128)(2,1)S(1)}, u32[]{:S(2)}, u32[]{:S(2)}) async-start(bf16[32,64,256]{2,1,0:T(8,128)(2,1)} %broadcast_in_dim.17), calls=%async_computation.1 | async-start | bytes 2097152 | tf_op jit(solution)/shard_map/all_to_all | solution.py:15
  127.5 20.7 %all-to-all-start.4 = ((bf16[32,64,128]{2,1,0:T(8,128)(2,1)}), bf16[32,64,128]{2,1,0:T(8,128)(2,1)S(1)}, u32[]{:S(2)}, u32[]{:S(2)}) async-start(bf16[32,64,128]{2,1,0:T(8,128)(2,1)} %constant_dynamic-update-slice_fusion), calls=%async_computation.4 | async-start | bytes 1048576 | tf_op jit(solution)/shard_map/all_to_all | solution.py:38
  148.1 1.6 copy-start.2
  149.7 3.9 %copy-start.4 = (f32[128,256]{1,0:T(8,128)S(1)}, f32[128,256]{1,0:T(8,128)}, u32[]{:S(2)}) copy-start(f32[128,256]{1,0:T(8,128)} %param.5) | copy-start | bytes 393220
  149.7 53.8 %all-to-all-start.2 = ((bf16[32,2,64,256]{3,2,1,0:T(8,128)(2,1)}), bf16[32,2,64,256]{3,2,1,0:T(8,128)(2,1)S(1)}, u32[]{:S(2)}, u32[]{:S(2)}) async-start(bf16[32,2,64,256]{3,2,1,0:T(8,128)(2,1)} %broadcast_in_dim.18), calls=%async_computation.2 | async-start | bytes 4194304 | tf_op jit(solution)/shard_map/all_to_all | solution.py:15
  267.3 5.8 %copy-start.1 = (bf16[16,64,256]{2,1,0:T(8,128)(2,1)S(1)}, bf16[16,64,256]{2,1,0:T(8,128)(2,1)}, u32[]{:S(2)}) copy-start(bf16[16,64,256]{2,1,0:T(8,128)(2,1)} %copy-done) | copy-start | bytes 1572868
  267.3 55.7 %all-to-all-start.6 = ((bf16[32,128,2,128]{3,1,2,0:T(8,128)(2,1)}), bf16[32,128,2,128]{3,1,2,0:T(8,128)(2,1)S(1)}, u32[]{:S(2)}, u32[]{:S(2)}) async-start(bf16[32,128,2,128]{3,1,2,0:T(8,128)(2,1)} %broadcast_in_dim.20), calls=%async_computation.6 | async-start | bytes 4194304 | tf_op jit(solution)/shard_map/all_to_all | solution.py:15
